TPU v7x, 256 devices: a whole 4x4x8 slice. The times are simulated.
256 devices in a mesh: row: 8 (over x, core), col: 32 (over z, y).
Axes of the slice: x: 4, y: 4, z: 8, core: 2. Of those that a mesh axis runs over, the one named last changes fastest.
Arguments:
- blocks: bfloat16 [12288, 27, 48, 48], P(('row', 'col')), may hold values from -0.59765625 to 0.59765625
- prolong: bfloat16 [12288, 48, 48], P(('row', 'col')), may hold values from -0.875 to 0.875
- columns: int32 [12288, 27], P(('row', 'col')), may hold values from 0 to 383
- aggregate: int32 [12288], P(('row', 'col')), may hold values from 0 to 15
- slots: int32 [12288, 27], P(('row', 'col')), may hold values from 0 to 26
Outputs:
- coarse: float32 [128, 27, 2304], P('row', None, 'col')
Inputs may be any that keep to these rules, and one draw needn't show every extreme that they name: `columns`: a fine block row's neighbours all lie in its column tile: the fine block rows of the devices with the same col index, in order of their row index.
All inputs are finite; a program needn't handle non-finite values.
Results may differ from a plain program's by a relative error of at most 0.0029.
Values may be sent and summed in bfloat16 or wider, within the bound.
No kernel may reach another device: no remote copies, remote signals or barrier semaphores. Data moves between devices by JAX's collectives and lax.ppermute only.
A program may use at most 192 MiB of HBM per device.

v0:
```python
import jax
import jax.numpy as jnp
from jax import lax
from jax.sharding import PartitionSpec as P

KC = 27
CR_SLAB = 16


def shards(blocks, prolong, columns, aggregate, slots):
    width = blocks.shape[2]
    tile = lax.all_gather(prolong, "row", axis=0, tiled=True)
    picked = jnp.take(tile, columns, axis=0)
    product = jnp.einsum(
        "rkab,rkbc->rkac", blocks, picked, preferred_element_type=jnp.float32
    ).astype(jnp.bfloat16)
    term = jnp.einsum("rba,rkbc->rkac", prolong, product, preferred_element_type=jnp.float32)
    target = (aggregate[:, None] * KC + slots).reshape(-1)
    partial_value = jax.ops.segment_sum(
        term.reshape(-1, width * width), target, num_segments=CR_SLAB * KC
    )
    partial_value = partial_value.reshape(CR_SLAB, KC, width * width)
    summed = lax.psum(partial_value, "col")
    share = width * width // lax.axis_size("col")
    result = lax.dynamic_slice_in_dim(summed, lax.axis_index("col") * share, share, 2)
    return result


def solution(mesh):
    return jax.shard_map(
        shards,
        mesh=mesh,
        in_specs=(
            P(("row", "col"), None, None, None),
            P(("row", "col"), None, None),
            P(("row", "col"), None),
            P(("row", "col")),
            P(("row", "col"), None),
        ),
        out_specs=P("row", None, "col"),
        check_vma=False,
    )
```

profile of v0, /device:TPU:2, one launch (start us, length us, event | category | flops | bytes accessed | tf_op | source)
XLA Modules:
  0.0 371.9 jit_solution(16122000803956569116)
XLA Ops:
  6.5 0.0 all-gather.2.cloned.1.call-start
  6.5 0.7 all-gather.2.cloned.1.call-update
  7.3 0.0 all-reduce.2.cloned.1.call-start
  7.3 0.7 compare_select_fusion
  8.0 0.1 copy.14
  8.1 0.1 reshape.17
  8.2 0.7 compare_and_fusion
  9.0 0.1 copy.13
  9.1 0.7 broadcast_multiply_fusion
  9.7 0.7 broadcast_add_fusion
  10.4 0.1 copy.12
  10.5 0.1 reshape.25
  10.7 37.4 %all-gather.2.cloned.1.call-done = bf16[384,48,48]{2,1,0:T(8,128)(2,1)} async-done(((bf16[48,48,48]{2,1,0:T(8,128)(2,1)}), bf16[384,48,48]{2,1,0:T(8,128)(2,1)}) %all-gather.2.cloned.1.call-update) | async-done | bytes 1769488 | tf_op jit(solution)/shard_map/all_gather | solution.py:12
  48.0 10.4 %gather_fusion = bf16[1296,48,48]{2,1,0:T(8,128)(2,1)} fusion(bf16[384,48,48]{2,1,0:T(8,128)(2,1)} %all-gather.2.cloned.1.call-done, s32[2048]{0:T(1024)S(1)} %pad_clamp_fusion), kind=kCustom, calls=%fused_computation | custom fusion | bytes 11949120 | tf_op jit(solution)/shard_map/jit(_take)/gather | solution.py:13
  58.5 22.0 %copy.15 = bf16[48,27,48,48]{2,3,1,0:T(8,128)(2,1)} copy(bf16[48,27,48,48]{3,2,1,0:T(8,128)(2,1)} %bitcast.16) | data formatting | bytes 11943936 | tf_op jit(solution)/shard_map/jit(_take)/gather | solution.py:13
  80.4 27.9 %fusion.10 = f32[48,27,48,48]{2,3,1,0:T(8,128)} fusion(bf16[48,27,48,48]{3,2,1,0:T(8,128)(2,1)} %param.5, bf16[48,27,48,48]{2,3,1,0:T(8,128)(2,1)} %copy.15, pred[48,27]{1,0:T(8,128)(4,1)S(1)} %copy.13, bf16[48,48,48]{2,1,0:T(8,128)(2,1)S(1)} %copy-done), kind=kOutput, calls=%fused_computation.8 | convolution fusion | flops 579280896 | bytes 24110352 | tf_op jit(solution)/shard_map/rba,rkbc->rkac/dot_general | solution.py:17
  108.3 32.6 %copy.16 = f32[48,27,48,48]{3,2,1,0:T(8,128)} copy(f32[48,27,48,48]{2,3,1,0:T(8,128)} %fusion.10) | data formatting | bytes 23887872 | tf_op jit(solution)/shard_map/rba,rkbc->rkac/transpose | solution.py:17
  140.9 25.7 %reshape.27 = f32[1296,2304]{1,0:T(8,128)} reshape(f32[48,27,48,48]{3,2,1,0:T(8,128)} %copy.16) | data formatting | bytes 23887872 | tf_op jit(solution)/shard_map/reshape | solution.py:20
  166.6 24.2 %scatter_custom_fusion = f32[432,2304]{1,0:T(8,128)} fusion(s32[1296]{0:T(1024)S(1)} %reshape.25, f32[1296,2304]{1,0:T(8,128)} %reshape.27, f32[]{:T(128)} %constant.9.clone.1), kind=kCustom, calls=%fused_computation.10 | custom fusion | flops 2985984 | bytes 3981824 | tf_op jit(solution)/shard_map/scatter-add | solution.py:19
  190.8 3.9 %reshape.14 = f32[16,27,2304]{2,1,0:T(8,128)} reshape(f32[432,2304]{1,0:T(8,128)} %scatter_custom_fusion) | data formatting | bytes 7962624 | tf_op jit(solution)/shard_map/reshape | solution.py:22
  194.7 0.0 all-reduce.2.cloned.1.call-update
  194.8 168.3 %all-reduce.2.cloned.1.call-done = f32[16,27,2304]{2,1,0:T(8,128)} async-done(((f32[16,27,2304]{2,1,0:T(8,128)}), f32[16,27,2304]{2,1,0:T(8,128)}) %all-reduce.2.cloned.1.call-update) | async-done | bytes 3981328 | tf_op jit(solution)/shard_map/psum | solution.py:23
  363.1 1.2 constant_dynamic-slice_fusion
  364.3 0.8 copy.17
  (3 shorter events, 0.0 us)
Async XLA Ops:
  6.5 41.5 %all-gather.2.cloned.1.call-start = ((), (), s32[]{:S(2)}) async-start(), calls=%async_computation | async-start | bytes 5308416 | tf_op jit(solution)/shard_map/all_gather | solution.py:12
  7.3 355.8 %all-reduce.2.cloned.1.call-start = ((), (), s32[]{:S(2)}) async-start(), calls=%async_computation.1 | async-start | bytes 9437184 | tf_op jit(solution)/shard_map/psum | solution.py:23
  58.5 22.0 %copy-start = (bf16[48,48,48]{2,1,0:T(8,128)(2,1)S(1)}, bf16[48,48,48]{2,1,0:T(8,128)(2,1)}, u32[]{:S(2)}) copy-start(bf16[48,48,48]{2,1,0:T(8,128)(2,1)} %param.6) | copy-start | bytes 663556
Sparse Core Ops, SparseCore 0:
  9.2 38.8 all-gather.1
  194.9 168.1 all-reduce.1
where the time goes:
time: 374 us; the launch traced here: 372 us
  waiting for transfers between devices  206 us (55%)
  local copies, waits for them, and re-layouts  97.1 us (26%)
  matrix products  27.9 us (7%)
  other arithmetic  27.1 us (7%)
  between operations  13.4 us (4%)
    psum x1, waiting for transfers between devices, shards(): summed = lax.psum(partial_value, 'col')  168 us
    all_gather x1, waiting for transfers between devices, shards(): tile = lax.all_gather(prolong, 'row', axis=0, tiled=True)  37.4 us
    transpose x1, local copies, waits for them, and re-layouts, shards(): jnp.einsum('rba,rkbc->rkac', prolong, product, preferred_element_type=jnp...  32.6 us
    gather x2, local copies, waits for them, and re-layouts, shards(): picked = jnp.take(tile, columns, axis=0)  32.4 us
    dot_general x1, matrix products, shards(): jnp.einsum('rba,rkbc->rkac', prolong, product, preferred_element_type=jnp...  27.9 us
    reshape x1, local copies, waits for them, and re-layouts, shards(): term.reshape(-1, width * width)  25.7 us
    scatter-add x1, other arithmetic, shards(): jax.ops.segment_sum(term.reshape(-1, width * width), target, num_segments...  24.2 us
  transfers between devices with their start and end apart: 2, of which 2 were waited for; matrix products, arithmetic and copies ran while one was open for 1% of the time, Pallas kernels for 0%

commit v1 on v0

--- a/solution.py
+++ b/solution.py
@@ -20,7 +20,7 @@
         term.reshape(-1, width * width), target, num_segments=CR_SLAB * KC
     )
     partial_value = partial_value.reshape(CR_SLAB, KC, width * width)
-    summed = lax.psum(partial_value, "col")
+    summed = jnp.sum(lax.all_gather(partial_value, axis_name="col"), axis=0)
     share = width * width // lax.axis_size("col")
     result = lax.dynamic_slice_in_dim(summed, lax.axis_index("col") * share, share, 2)
     return result

time: 374 us -> 1040 us (2.78)
  waiting for transfers between devices: 206 us -> 827 us
  other arithmetic: 27.1 us -> 67.7 us
    all_gather x0 -> x1, waiting for transfers between devices: none -> 789 us  [shards(): summed = jnp.sum(lax.all_gather(partial_value, axis_name='col'), axis=0)]
    psum x1 -> x0, waiting for transfers between devices: 168 us -> none  [shards(): summed = lax.psum(partial_value, 'col')]
    reduce_sum x0 -> x1, other arithmetic: none -> 40.7 us  [shards(): summed = jnp.sum(lax.all_gather(partial_value, axis_name='col'), axis=0)]
    another operation x0 -> x2, local copies, waits for them, and re-layouts: none -> 10.5 us  [shards(): summed = jnp.sum(lax.all_gather(partial_value, axis_name='col'), axis=0)]
  transfers between devices with their start and end apart: 2 -> 2, of which waited for: 2 -> 2; matrix products, arithmetic and copies ran while one was open for 1% -> 0% of each run, Pallas kernels for 0% -> 0%
where the time goes in v1:
time: 1040 us
  waiting for transfers between devices  827 us (80%)
  local copies, waits for them, and re-layouts  104 us (10%)
  other arithmetic  67.7 us (7%)
  matrix products  27.9 us (3%)
  between operations  13.4 us (1%)
    all_gather x1, waiting for transfers between devices, shards(): summed = jnp.sum(lax.all_gather(partial_value, axis_name='col'), axis=0)  789 us
    reduce_sum x1, other arithmetic, shards(): summed = jnp.sum(lax.all_gather(partial_value, axis_name='col'), axis=0)  40.7 us
    all_gather x1, waiting for transfers between devices, shards(): tile = lax.all_gather(prolong, 'row', axis=0, tiled=True)  37.4 us
    transpose x1, local copies, waits for them, and re-layouts, shards(): jnp.einsum('rba,rkbc->rkac', prolong, product, preferred_element_type=jnp...  32.6 us
    gather x2, local copies, waits for them, and re-layouts, shards(): picked = jnp.take(tile, columns, axis=0)  32.4 us
    dot_general x1, matrix products, shards(): jnp.einsum('rba,rkbc->rkac', prolong, product, preferred_element_type=jnp...  27.9 us
    reshape x1, local copies, waits for them, and re-layouts, shards(): term.reshape(-1, width * width)  25.7 us
    scatter-add x1, other arithmetic, shards(): jax.ops.segment_sum(term.reshape(-1, width * width), target, num_segments...  24.2 us
  transfers between devices with their start and end apart: 2, of which 2 were waited for; matrix products, arithmetic and copies ran while one was open for 0% of the time, Pallas kernels for 0%

profile of v1, /device:TPU:2, one launch (start us, length us, event | category | flops | bytes accessed | tf_op | source)
XLA Modules:
  0.0 1039.3 jit_solution(10401584587145015999)
XLA Ops:
  6.5 0.7 all-gather.3.cloned.1.call-update
  7.3 0.0 all-gather.5.cloned.1.call-start
  7.3 0.7 broadcast_multiply_fusion
  8.0 0.7 broadcast_add_fusion
  8.7 0.1 copy.11
  8.8 0.1 reshape.21
  8.9 0.7 compare_select_fusion
  9.6 0.1 copy.13
  9.7 0.1 reshape.13
  9.8 0.7 compare_and_fusion
  10.6 0.1 copy.12
  10.7 37.4 %all-gather.3.cloned.1.call-done = bf16[384,48,48]{2,1,0:T(8,128)(2,1)} async-done(((bf16[48,48,48]{2,1,0:T(8,128)(2,1)}), bf16[384,48,48]{2,1,0:T(8,128)(2,1)}) %all-gather.3.cloned.1.call-update) | async-done | bytes 1769488 | tf_op jit(solution)/shard_map/all_gather | solution.py:12
  48.0 10.4 %gather_fusion = bf16[1296,48,48]{2,1,0:T(8,128)(2,1)} fusion(bf16[384,48,48]{2,1,0:T(8,128)(2,1)} %all-gather.3.cloned.1.call-done, s32[2048]{0:T(1024)S(1)} %pad_clamp_fusion), kind=kCustom, calls=%fused_computation | custom fusion | bytes 11949120 | tf_op jit(solution)/shard_map/jit(_take)/gather | solution.py:13
  58.5 22.0 %copy.14 = bf16[48,27,48,48]{2,3,1,0:T(8,128)(2,1)} copy(bf16[48,27,48,48]{3,2,1,0:T(8,128)(2,1)} %bitcast.16) | data formatting | bytes 11943936 | tf_op jit(solution)/shard_map/jit(_take)/gather | solution.py:13
  80.4 27.9 %fusion.10 = f32[48,27,48,48]{2,3,1,0:T(8,128)} fusion(bf16[48,27,48,48]{3,2,1,0:T(8,128)(2,1)} %param.5, bf16[48,27,48,48]{2,3,1,0:T(8,128)(2,1)} %copy.14, pred[48,27]{1,0:T(8,128)(4,1)S(1)} %copy.12, bf16[48,48,48]{2,1,0:T(8,128)(2,1)S(1)} %copy-done), kind=kOutput, calls=%fused_computation.8 | convolution fusion | flops 579280896 | bytes 24110352 | tf_op jit(solution)/shard_map/rba,rkbc->rkac/dot_general | solution.py:17
  108.3 32.6 %copy.15 = f32[48,27,48,48]{3,2,1,0:T(8,128)} copy(f32[48,27,48,48]{2,3,1,0:T(8,128)} %fusion.10) | data formatting | bytes 23887872 | tf_op jit(solution)/shard_map/rba,rkbc->rkac/transpose | solution.py:17
  140.9 25.7 %reshape.23 = f32[1296,2304]{1,0:T(8,128)} reshape(f32[48,27,48,48]{3,2,1,0:T(8,128)} %copy.15) | data formatting | bytes 23887872 | tf_op jit(solution)/shard_map/reshape | solution.py:20
  166.6 24.2 %scatter_custom_fusion = f32[432,2304]{1,0:T(8,128)} fusion(s32[1296]{0:T(1024)S(1)} %reshape.21, f32[1296,2304]{1,0:T(8,128)} %reshape.23, f32[]{:T(128)} %constant.9.clone.1), kind=kCustom, calls=%fused_computation.10 | custom fusion | flops 2985984 | bytes 3981824 | tf_op jit(solution)/shard_map/scatter-add | solution.py:19
  190.8 3.9 all_gather_reshape.3
  194.7 6.6 copy.16
  201.3 0.0 all-gather.5.cloned.1.call-update
  201.4 788.6 %all-gather.5.cloned.1.call-done = f32[32,16,27,2304]{3,1,2,0:T(8,128)} async-done(((f32[1,16,27,2304]{3,1,2,0:T(8,128)}), f32[32,16,27,2304]{3,1,2,0:T(8,128)}) %all-gather.5.cloned.1.call-update) | async-done | bytes 127402000 | tf_op jit(solution)/shard_map/all_gather | solution.py:23
  989.9 40.7 %reduce_sum.9 = f32[16,27,2304]{2,0,1:T(8,128)} reduce(f32[32,16,27,2304]{3,1,2,0:T(8,128)} %all-gather.5.cloned.1.call-done, f32[]{:T(128)} %constant.9.clone.1), dimensions={0}, to_apply=%region_1.2 | reduce | flops 30855168 | bytes 131383296 | tf_op jit(solution)/shard_map/reduce_sum | solution.py:23
  1030.6 1.8 constant_dynamic-slice_fusion
  (4 shorter events, 0.0 us)
Async XLA Ops:
  6.5 41.5 %all-gather.3.cloned.1.call-start = ((), (), s32[]{:S(2)}) async-start(), calls=%async_computation | async-start | bytes 5308416 | tf_op jit(solution)/shard_map/all_gather | solution.py:12
  7.3 982.7 %all-gather.5.cloned.1.call-start = ((), (), s32[]{:S(2)}) async-start(), calls=%async_computation.1 | async-start | bytes 131383296 | tf_op jit(solution)/shard_map/all_gather | solution.py:23
  58.5 22.0 %copy-start = (bf16[48,48,48]{2,1,0:T(8,128)(2,1)S(1)}, bf16[48,48,48]{2,1,0:T(8,128)(2,1)}, u32[]{:S(2)}) copy-start(bf16[48,48,48]{2,1,0:T(8,128)(2,1)} %param.6) | copy-start | bytes 663556
Sparse Core Ops, SparseCore 0:
  9.2 38.8 all-gather.2
  201.5 788.4 all-gather.4
